TPU v7x, 32 devices: a whole 2x2x4 slice. The times are simulated.
32 devices in a mesh: tile: 16 (over z, y, x), mode: 2 (over core).
Axes of the slice: x: 2, y: 2, z: 4, core: 2. Of those that a mesh axis runs over, the one named last changes fastest.
Arguments:
- obj: float32 [16, 2, 384, 384], P('tile'), may hold values from -6 to 6
- probe: float32 [4, 2, 256, 256], P('mode'), may hold values from -3 to 3
- mode_weights: float32 [8, 4], P(None, 'mode'), may hold values from 0.25 to 1
- measured: float32 [64, 256, 256], P('tile'), may hold values from 0 to 4
- corner: int32 [64, 2], P('tile'), may hold values from 0 to 383, as said below
- counts: int32 [16], P('tile'), may hold values from 1 to 4, 32 in all
- weight_index: int32 [64], P('tile'), may hold values from 0 to 7
Outputs:
- obj_new: float32 [16, 2, 384, 384], P('tile')
- probe_new: float32 [4, 2, 256, 256], P('mode')
Inputs may be any that keep to these rules, and one draw needn't show every extreme that they name: Tile t has live slots 0 to counts[t] - 1 of its block; the counts sum to 32 and some tile has 4. The first slot of every tile has both corner coordinates between 192 and 320.
All inputs are finite; a program needn't handle non-finite values.
Results may differ from a plain program's by a relative error of at most 0.019.
The roundings to bfloat16 on the way count: a program that leaves them out, or rounds other values in their place, can miss the bound.
Values may be sent and summed in bfloat16 or wider, within the bound.
No kernel may reach another device: no remote copies, remote signals or barrier semaphores. Data moves between devices by JAX's collectives and lax.ppermute only.
A program may use at most 64 MiB of HBM per device.

v0:
```python
import math
import jax
import jax.numpy as jnp
from jax import lax
from jax.sharding import PartitionSpec as P

GC = 8
POS_DEV = 2
ITERS = 2
step_object = 0.1
step_probe = 4.0


def shifted(array, axis, by):
    peers = lax.axis_size(axis)
    return lax.ppermute(array, axis, [(i, (i + by) % peers) for i in range(peers)])


def dft_tables(length, sign):
    index = jnp.arange(length, dtype=jnp.int32)
    product = index[:, None] * index[None, :] % length
    angle = product.astype(jnp.float32) * (2.0 * math.pi / length)
    factor = 1.0 / math.sqrt(length)
    real = jnp.cos(angle) * factor
    imag = sign * jnp.sin(angle) * factor
    left = jnp.concatenate(
        [jnp.concatenate([real, -imag], 1), jnp.concatenate([imag, real], 1)], 0
    ).astype(jnp.bfloat16)
    right = jnp.concatenate([real, imag], 1).astype(jnp.bfloat16)
    return (left, right)


def transform(field, tables):
    left, right = tables
    count = field.shape[0]
    length = field.shape[-1]
    first = jnp.einsum(
        "ij,bjk->bik",
        left,
        field.reshape(count, 2 * length, length),
        preferred_element_type=jnp.float32,
    )
    first = first.astype(jnp.bfloat16).reshape(count, 2, length, length)
    second = jnp.einsum("bcjk,kl->bcjl", first, right, preferred_element_type=jnp.float32)
    real = second[:, 0, :, :length] - second[:, 1, :, length:]
    imag = second[:, 0, :, length:] + second[:, 1, :, :length]
    return jnp.stack([real, imag], 1)


def patch_contributions(
    object_patches, measured, active_mask, mode_weighting, probe, forward_pass, backward_pass, total
):
    count = object_patches.shape[0]
    modes = probe.shape[0]
    length = probe.shape[-1]
    obj_part = object_patches.astype(jnp.float32)[:, None]
    probe_part = probe[None]
    exit_real = probe_part[:, :, 0] * obj_part[:, :, 0] - probe_part[:, :, 1] * obj_part[:, :, 1]
    exit_imag = probe_part[:, :, 0] * obj_part[:, :, 1] + probe_part[:, :, 1] * obj_part[:, :, 0]
    exit_wave = jnp.stack([exit_real, exit_imag], 2).astype(jnp.bfloat16)
    psi = transform(exit_wave.reshape(count * modes, 2, length, length), forward_pass).reshape(
        count, modes, 2, length, length
    )
    power = psi[:, :, 0] * psi[:, :, 0] + psi[:, :, 1] * psi[:, :, 1]
    intensity = total(jnp.sum(mode_weighting[:, :, None, None] * power, 1))
    resid = (intensity - measured) * active_mask[:, None, None]
    scaled = (mode_weighting[:, :, None, None, None] * resid[:, None, None] * psi).astype(
        jnp.bfloat16
    )
    chi = transform(scaled.reshape(count * modes, 2, length, length), backward_pass).reshape(
        count, modes, 2, length, length
    )
    obj_real = jnp.sum(probe_part[:, :, 0] * chi[:, :, 0] + probe_part[:, :, 1] * chi[:, :, 1], 1)
    obj_imag = jnp.sum(probe_part[:, :, 0] * chi[:, :, 1] - probe_part[:, :, 1] * chi[:, :, 0], 1)
    probe_real = jnp.sum(obj_part[:, :, 0] * chi[:, :, 0] + obj_part[:, :, 1] * chi[:, :, 1], 0)
    probe_imag = jnp.sum(obj_part[:, :, 0] * chi[:, :, 1] - obj_part[:, :, 1] * chi[:, :, 0], 0)
    return (jnp.stack([obj_real, obj_imag], 1), jnp.stack([probe_real, probe_imag], 1))


def unchanged(value):
    return value


def body(obj, probe, mode_weights, measured, corner, counts, weight_index):
    patch = probe.shape[-1]
    tile = obj.shape[-1]
    capacity = measured.shape[0]
    kinds = mode_weights.shape[0]
    zero_index = jnp.zeros((), jnp.int32)
    forward_pass = dft_tables(patch, -1.0)
    backward_pass = dft_tables(patch, 1.0)
    active_mask = (jnp.arange(capacity, dtype=jnp.int32) < counts[0]).astype(jnp.float32)
    onehot = (weight_index[:, None] == jnp.arange(kinds, dtype=jnp.int32)[None, :]).astype(
        jnp.float32
    )
    positions = POS_DEV * lax.axis_size("tile")
    state = obj[0]
    probe_now = probe
    for sweep in range(ITERS):
        half = state.astype(jnp.bfloat16)
        right = shifted(half[:, :, :patch], "tile", -1)
        wide = jnp.concatenate([half, right], 2)
        below = shifted(half[:, :patch, :], "tile", -GC)
        diagonal = shifted(half[:, :patch, :patch], "tile", -(GC + 1))
        lower = jnp.concatenate([below, diagonal], 2)
        padded = jnp.concatenate([wide, lower], 1)

        def cut(spot):
            return lax.dynamic_slice(padded, (zero_index, spot[0], spot[1]), (2, patch, patch))

        object_patches = jax.vmap(cut)(corner)
        groups = lax.axis_size("mode")
        mine = lax.axis_index("mode")

        def pick(array):
            shaped = array.reshape((capacity // groups, groups) + array.shape[1:])
            return lax.dynamic_index_in_dim(shaped, mine, 1, keepdims=False)

        all_probe, all_weights = (
            lax.all_gather(probe_now, "mode", axis=0, tiled=True),
            lax.all_gather(mode_weights, "mode", axis=1, tiled=True),
        )
        mode_weighting = jnp.dot(pick(onehot), all_weights, precision=lax.Precision.HIGHEST)
        object_terms, probe_updates = patch_contributions(
            pick(object_patches),
            pick(measured),
            pick(active_mask),
            mode_weighting,
            all_probe,
            forward_pass,
            backward_pass,
            unchanged,
        )
        probe_updates = lax.psum_scatter(
            probe_updates.astype(jnp.bfloat16), "mode", scatter_dimension=0, tiled=True
        ).astype(jnp.float32)
        slot_corner = pick(corner)

        def place(slot, acc):
            spot = slot_corner[slot]
            where = (zero_index, spot[0], spot[1])
            current = lax.dynamic_slice(acc, where, (2, patch, patch))
            return lax.dynamic_update_slice(acc, current + object_terms[slot], where)

        gradient = jnp.zeros((2, tile + patch, tile + patch), jnp.float32)
        gradient = lax.fori_loop(0, object_terms.shape[0], place, gradient)
        above = shifted(gradient[:, tile:, :tile].astype(jnp.bfloat16), "tile", GC).astype(
            jnp.float32
        )
        upper_left = shifted(gradient[:, tile:, tile:].astype(jnp.bfloat16), "tile", GC + 1).astype(
            jnp.float32
        )
        gradient = gradient.at[:, :patch, :tile].add(above)
        gradient = gradient.at[:, :patch, :patch].add(upper_left)
        from_left = shifted(gradient[:, :tile, tile:].astype(jnp.bfloat16), "tile", 1).astype(
            jnp.float32
        )
        tile_grad = gradient[:, :tile, :tile].at[:, :, :patch].add(from_left)
        tile_grad = lax.psum(tile_grad.astype(jnp.bfloat16), "mode").astype(jnp.float32)
        probe_grad = lax.psum(probe_updates, "tile")
        state = state - step_object * tile_grad
        probe_now = probe_now - step_probe / positions * probe_grad
    return (state[None], probe_now)


def solution(mesh):
    placed = (
        P("tile", None, None, None),
        P("mode", None, None, None),
        P(None, "mode"),
        P("tile", None, None),
        P("tile", None),
        P("tile"),
        P("tile"),
    )
    return jax.shard_map(
        body,
        mesh=mesh,
        in_specs=placed,
        out_specs=(P("tile", None, None, None), P("mode", None, None, None)),
        check_vma=False,
    )
```

profile of v0, /device:TPU:0, one launch (start us, length us, event | category | flops | bytes accessed | tf_op | source)
XLA Modules:
  0.0 576.5 jit_solution(13252138141887793834)
XLA Ops:
  8.6 7.0 %collective-permute-start = (bf16[2,384,256]{2,1,0:T(8,128)(2,1)S(1)}, bf16[2,384,256]{2,1,0:T(8,128)(2,1)S(1)}, u32[]{:S(2)}, u32[]{:S(2)}) collective-permute-start(bf16[2,384,256]{2,1,0:T(8,128)(2,1)S(1)} %slice.449), channel_id=1, source_target_pairs={{0,30},{2,0},{4,2},{6,4},{8,6},{10,8},{12,10},{14,12},{16,14},{18,... | collective-permute-start | bytes 1179656 | tf_op jit(solution)/shard_map/ppermute | solution.py:16
  25.1 17.7 %collective-permute-done.2 = bf16[2,256,256]{2,1,0:T(8,128)(2,1)S(1)} collective-permute-done((bf16[2,256,256]{2,1,0:T(8,128)(2,1)S(1)}, bf16[2,256,256]{2,1,0:T(8,128)(2,1)S(1)}, u32[]{:S(2)}, u32[]{:S(2)}) %collective-permute-start.2) | collective-permute-done | bytes 262176 | tf_op jit(solution)/shard_map/ppermute | solution.py:16
  46.6 8.3 %while.36 = (s32[]{:T(128)}, bf16[2,640,640]{2,1,0:T(8,128)(2,1)S(1)}, s32[4,3]{1,0:T(4,128)S(1)}, bf16[4,2,256,256]{3,2,1,0:T(8,128)(2,1)S(1)}, s32[]{:T(128)}) while((s32[]{:T(128)}, bf16[2,640,640]{2,1,0:T(8,128)(2,1)S(1)}, s32[4,3]{1,0:T(4,128)S(1)}, bf16[4,2,256,256]{3,2,1,0:T(8,128)(2,1)S(1)}, s32[]{:T(128)}) %tuple.139), condition=%wide.while_cond.6, body=%wide.while_body.6.sunk | while | flops 2 | bytes 524405 | solution.py:109
  60.8 5.5 subtract_convert_fusion.1
  107.6 24.8 %while.34 = (s32[]{:T(128)}, f32[2,640,640]{2,1,0:T(8,128)}, s32[2,2]{1,0:T(2,128)S(1)}, f32[2,2,256,256]{3,2,1,0:T(8,128)S(1)}, s32[]{:T(128)}, /*index=5*/s32[]{:T(128)}, s32[]{:T(128)}) while((s32[]{:T(128)}, f32[2,640,640]{2,1,0:T(8,128)}, s32[2,2]{1,0:T(2,128)S(1)}, f32[2,2,256,256]{3,2,1,0:T(8,128)S(1)}, s32[]{:T(128)}, ...), condition=%wide.region_4.5_spmd, body=%wide.region_3.4_spmd.sunk | while | flops 131080 | bytes 2621637 | solution.py:146
  113.5 6.3 %dynamic_update_slice.16 = f32[2,640,640]{2,1,0:T(8,128)} dynamic-update-slice(f32[2,640,640]{2,1,0:T(8,128)} %get-tuple-element.475, f32[2,256,256]{2,1,0:T(8,128)S(1)} %bitcast_add_fusion.4, s32[]{:T(128)} %constant.258.clone.1..sunk, s32[]{:T(128)S(6)} %select_n.129, s32[]{:T(128)S(6)} %select_n.130) | dynamic-update-slice | bytes 1048580 | tf_op jit(solution)/shard_map/while/body/eval_jaxpr/dynamic_update_slice | solution.py:143
  125.7 6.8 %dynamic_update_slice.16 = f32[2,640,640]{2,1,0:T(8,128)} dynamic-update-slice(f32[2,640,640]{2,1,0:T(8,128)} %get-tuple-element.475, f32[2,256,256]{2,1,0:T(8,128)S(1)} %bitcast_add_fusion.4, s32[]{:T(128)} %constant.258.clone.1..sunk, s32[]{:T(128)S(6)} %select_n.129, s32[]{:T(128)S(6)} %select_n.130) | dynamic-update-slice | bytes 1048580 | tf_op jit(solution)/shard_map/while/body/eval_jaxpr/dynamic_update_slice | solution.py:143
  136.1 24.7 %collective-permute-done.3 = bf16[2,256,384]{2,1,0:T(8,128)(2,1)S(1)} collective-permute-done((bf16[2,256,384]{2,1,0:T(8,128)(2,1)S(1)}, bf16[2,256,384]{2,1,0:T(8,128)(2,1)S(1)}, u32[]{:S(2)}, u32[]{:S(2)}) %collective-permute-start.3) | collective-permute-done | bytes 393248 | tf_op jit(solution)/shard_map/ppermute | solution.py:16
  161.2 5.9 %collective-permute-start.5 = (bf16[2,384,256]{2,1,0:T(8,128)(2,1)S(1)}, bf16[2,384,256]{2,1,0:T(8,128)(2,1)S(1)}, u32[]{:S(2)}, u32[]{:S(2)}) collective-permute-start(bf16[2,384,256]{2,1,0:T(8,128)(2,1)S(1)} %slice.531), channel_id=1, source_target_pairs={{0,2},{2,4},{4,6},{6,8},{8,10},{10,12},{12,14},{14,16},{16,18},{18... | collective-permute-start | bytes 1179656 | tf_op jit(solution)/shard_map/ppermute | solution.py:16
  167.2 7.6 %collective-permute-done.5 = bf16[2,384,256]{2,1,0:T(8,128)(2,1)S(1)} collective-permute-done((bf16[2,384,256]{2,1,0:T(8,128)(2,1)S(1)}, bf16[2,384,256]{2,1,0:T(8,128)(2,1)S(1)}, u32[]{:S(2)}, u32[]{:S(2)}) %collective-permute-start.5) | collective-permute-done | bytes 393248 | tf_op jit(solution)/shard_map/ppermute | solution.py:16
  176.9 17.3 %all-reduce.5.cloned.1.call-done = bf16[2,384,384]{2,1,0:T(8,128)(2,1)} async-done(((bf16[2,384,384]{2,1,0:T(8,128)(2,1)}), bf16[2,384,384]{2,1,0:T(8,128)(2,1)}) %all-reduce.5.cloned.1.call-update) | async-done | bytes 589840 | tf_op jit(solution)/shard_map/psum | solution.py:159
  197.8 5.4 collective-permute-start.6
  206.7 103.1 %all-reduce.8 = f32[2,2,256,256]{3,2,1,0:T(8,128)} all-reduce(bf16[2,2,256,256]{3,2,1,0:T(8,128)(2,1)} %reduce-scatter.3.cloned.1.call-done), channel_id=1, replica_groups=mesh['tile'=16,'mode'=2] {'tile'}, use_global_device_ids=true, to_apply=%region_9.10 | all-reduce | flops 262144 | bytes 1572864 | tf_op jit(solution)/shard_map/psum | solution.py:160
  315.4 11.3 %while.37 = (s32[]{:T(128)}, bf16[2,640,640]{2,1,0:T(8,128)(2,1)S(1)}, s32[4,3]{1,0:T(4,128)S(1)}, bf16[4,2,256,256]{3,2,1,0:T(8,128)(2,1)}, s32[]{:T(128)}) while((s32[]{:T(128)}, bf16[2,640,640]{2,1,0:T(8,128)(2,1)S(1)}, s32[4,3]{1,0:T(4,128)S(1)}, bf16[4,2,256,256]{3,2,1,0:T(8,128)(2,1)}, s32[]{:T(128)}) %tuple.163), condition=%wide.while_cond.7, body=%wide.while_body.7.sunk | while | flops 2 | bytes 525929 | solution.py:109
  334.9 5.7 subtract_convert_fusion
  382.9 24.8 %while.35 = (s32[]{:T(128)}, f32[2,640,640]{2,1,0:T(8,128)}, s32[2,2]{1,0:T(2,128)S(1)}, f32[2,2,256,256]{3,2,1,0:T(8,128)S(1)}, s32[]{:T(128)}, /*index=5*/s32[]{:T(128)}, s32[]{:T(128)}) while((s32[]{:T(128)}, f32[2,640,640]{2,1,0:T(8,128)}, s32[2,2]{1,0:T(2,128)S(1)}, f32[2,2,256,256]{3,2,1,0:T(8,128)S(1)}, s32[]{:T(128)}, ...), condition=%wide.region_14.15_spmd, body=%wide.region_13.14_spmd.sunk | while | flops 131080 | bytes 2621637 | solution.py:146
  388.7 6.3 %dynamic_update_slice.17 = f32[2,640,640]{2,1,0:T(8,128)} dynamic-update-slice(f32[2,640,640]{2,1,0:T(8,128)} %get-tuple-element.511, f32[2,256,256]{2,1,0:T(8,128)S(1)} %bitcast_add_fusion.5, s32[]{:T(128)} %constant.258.clone.1..sunk.1, s32[]{:T(128)S(6)} %select_n.131, s32[]{:T(128)S(6)} %select_n.132) | dynamic-update-slice | bytes 1048580 | tf_op jit(solution)/shard_map/while/body/eval_jaxpr/dynamic_update_slice | solution.py:143
  400.9 6.8 %dynamic_update_slice.17 = f32[2,640,640]{2,1,0:T(8,128)} dynamic-update-slice(f32[2,640,640]{2,1,0:T(8,128)} %get-tuple-element.511, f32[2,256,256]{2,1,0:T(8,128)S(1)} %bitcast_add_fusion.5, s32[]{:T(128)} %constant.258.clone.1..sunk.1, s32[]{:T(128)S(6)} %select_n.131, s32[]{:T(128)S(6)} %select_n.132) | dynamic-update-slice | bytes 1048580 | tf_op jit(solution)/shard_map/while/body/eval_jaxpr/dynamic_update_slice | solution.py:143
  410.7 17.1 %collective-permute-done.9 = bf16[2,256,384]{2,1,0:T(8,128)(2,1)S(1)} collective-permute-done((bf16[2,256,384]{2,1,0:T(8,128)(2,1)S(1)}, bf16[2,256,384]{2,1,0:T(8,128)(2,1)S(1)}, u32[]{:S(2)}, u32[]{:S(2)}) %collective-permute-start.9) | collective-permute-done | bytes 393248 | tf_op jit(solution)/shard_map/ppermute | solution.py:16
  428.2 5.5 collective-permute-start.11
  433.8 13.2 %collective-permute-done.11 = bf16[2,384,256]{2,1,0:T(8,128)(2,1)S(1)} collective-permute-done((bf16[2,384,256]{2,1,0:T(8,128)(2,1)S(1)}, bf16[2,384,256]{2,1,0:T(8,128)(2,1)S(1)}, u32[]{:S(2)}, u32[]{:S(2)}) %collective-permute-start.11) | collective-permute-done | bytes 393248 | tf_op jit(solution)/shard_map/ppermute | solution.py:16
  449.1 15.8 %all-reduce.7.cloned.1.call-done = bf16[2,384,384]{2,1,0:T(8,128)(2,1)} async-done(((bf16[2,384,384]{2,1,0:T(8,128)(2,1)}), bf16[2,384,384]{2,1,0:T(8,128)(2,1)}) %all-reduce.7.cloned.1.call-update) | async-done | bytes 589840 | tf_op jit(solution)/shard_map/psum | solution.py:159
  467.2 10.0 %reduce-scatter.5.cloned.1.call-done = bf16[2,2,256,256]{3,2,1,0:T(8,128)(2,1)} async-done(((bf16[4,2,256,256]{3,2,1,0:T(8,128)(2,1)}), bf16[2,2,256,256]{3,2,1,0:T(8,128)(2,1)}) %reduce-scatter.5.cloned.1.call-update) | async-done | bytes 524304 | tf_op jit(solution)/shard_map/reduce_scatter | solution.py:134
  477.2 91.1 %all-reduce.9 = f32[2,2,256,256]{3,2,1,0:T(8,128)S(1)} all-reduce(bf16[2,2,256,256]{3,2,1,0:T(8,128)(2,1)} %reduce-scatter.5.cloned.1.call-done), channel_id=1, replica_groups=mesh['tile'=16,'mode'=2] {'tile'}, use_global_device_ids=true, to_apply=%region_19.20 | all-reduce | flops 262144 | bytes 1572864 | tf_op jit(solution)/shard_map/psum | solution.py:160
  (242 shorter events, 166.0 us)
Async XLA Ops:
  7.2 50.2 %all-gather.4.cloned.1.call-start = ((), (), s32[]{:S(2)}) async-start(), calls=%async_computation.2 | async-start | bytes 3145728 | tf_op jit(solution)/shard_map/all_gather | solution.py:120
  8.6 34.2 %collective-permute-start = (bf16[2,384,256]{2,1,0:T(8,128)(2,1)S(1)}, bf16[2,384,256]{2,1,0:T(8,128)(2,1)S(1)}, u32[]{:S(2)}, u32[]{:S(2)}) collective-permute-start(bf16[2,384,256]{2,1,0:T(8,128)(2,1)S(1)} %slice.449), channel_id=1, source_target_pairs={{0,30},{2,0},{4,2},{6,4},{8,6},{10,8},{12,10},{14,12},{16,14},{18,... | collective-permute-start | bytes 1179656 | tf_op jit(solution)/shard_map/ppermute | solution.py:16
  15.7 30.7 %collective-permute-start.1 = (bf16[2,256,384]{2,1,0:T(8,128)(2,1)S(1)}, bf16[2,256,384]{2,1,0:T(8,128)(2,1)S(1)}, u32[]{:S(2)}, u32[]{:S(2)}) collective-permute-start(bf16[2,256,384]{2,1,0:T(8,128)(2,1)S(1)} %slice.450), channel_id=1, source_target_pairs={{0,16},{2,18},{4,20},{6,22},{8,24},{10,26},{12,28},{14,30},{16,0},... | collective-permute-start | bytes 1179656 | tf_op jit(solution)/shard_map/ppermute | solution.py:16
  15.8 27.0 %collective-permute-start.2 = (bf16[2,256,256]{2,1,0:T(8,128)(2,1)S(1)}, bf16[2,256,256]{2,1,0:T(8,128)(2,1)S(1)}, u32[]{:S(2)}, u32[]{:S(2)}) collective-permute-start(bf16[2,256,256]{2,1,0:T(8,128)(2,1)S(1)} %slice.451), channel_id=1, source_target_pairs={{0,14},{2,16},{4,18},{6,20},{8,22},{10,24},{12,26},{14,28},{16,30}... | collective-permute-start | bytes 786440 | tf_op jit(solution)/shard_map/ppermute | solution.py:16
  16.9 177.3 %all-reduce.5.cloned.1.call-start = ((), (), s32[]{:S(2)}) async-start(), calls=%async_computation.3 | async-start | bytes 1179648 | tf_op jit(solution)/shard_map/psum | solution.py:159
  19.7 61.1 %copy-start.24 = (bf16[256,256]{1,0:T(8,128)(2,1)}, bf16[256,256]{1,0:T(8,128)(2,1)S(1)}, u32[]{:S(2)}) copy-start(bf16[256,256]{1,0:T(8,128)(2,1)S(1)} %multiply_convert_fusion.2) | copy-start | bytes 393220
  132.5 28.4 %copy-start.1 = (f32[2,640,640]{2,1,0:T(8,128)S(1)}, f32[2,640,640]{2,1,0:T(8,128)}, u32[]{:S(2)}) copy-start(f32[2,640,640]{2,1,0:T(8,128)} %get-tuple-element.232) | copy-start | bytes 9830404
  134.8 26.1 %collective-permute-start.3 = (bf16[2,256,384]{2,1,0:T(8,128)(2,1)S(1)}, bf16[2,256,384]{2,1,0:T(8,128)(2,1)S(1)}, u32[]{:S(2)}, u32[]{:S(2)}) collective-permute-start(bf16[2,256,384]{2,1,0:T(8,128)(2,1)S(1)} %slice.463), channel_id=1, source_target_pairs={{0,16},{2,18},{4,20},{6,22},{8,24},{10,26},{12,28},{14,30},{16,0},... | collective-permute-start | bytes 1179656 | tf_op jit(solution)/shard_map/ppermute | solution.py:16
  134.9 26.2 %collective-permute-start.4 = (bf16[2,256,256]{2,1,0:T(8,128)(2,1)S(1)}, bf16[2,256,256]{2,1,0:T(8,128)(2,1)S(1)}, u32[]{:S(2)}, u32[]{:S(2)}) collective-permute-start(bf16[2,256,256]{2,1,0:T(8,128)(2,1)S(1)} %slice.465), channel_id=1, source_target_pairs={{0,18},{2,20},{4,22},{6,24},{8,26},{10,28},{12,30},{14,0},{16,2},{... | collective-permute-start | bytes 786440 | tf_op jit(solution)/shard_map/ppermute | solution.py:16
  161.2 13.6 %collective-permute-start.5 = (bf16[2,384,256]{2,1,0:T(8,128)(2,1)S(1)}, bf16[2,384,256]{2,1,0:T(8,128)(2,1)S(1)}, u32[]{:S(2)}, u32[]{:S(2)}) collective-permute-start(bf16[2,384,256]{2,1,0:T(8,128)(2,1)S(1)} %slice.531), channel_id=1, source_target_pairs={{0,2},{2,4},{4,6},{6,8},{8,10},{10,12},{12,14},{14,16},{16,18},{18... | collective-permute-start | bytes 1179656 | tf_op jit(solution)/shard_map/ppermute | solution.py:16
  175.8 31.0 %reduce-scatter.3.cloned.1.call-start = ((), (), s32[]{:S(2)}) async-start(), calls=%async_computation.4 | async-start | bytes 1572864 | tf_op jit(solution)/shard_map/reduce_scatter | solution.py:134
  176.9 153.3 %all-gather.6.cloned.1.call-start = ((), (), s32[]{:S(2)}) async-start(), calls=%async_computation.5 | async-start | bytes 3145728 | tf_op jit(solution)/shard_map/all_gather | solution.py:120
  195.5 114.3 %copy-start.18 = (f32[2,2,256,256]{3,2,1,0:T(8,128)S(1)}, f32[2,2,256,256]{3,2,1,0:T(8,128)}, u32[]{:S(2)}) copy-start(f32[2,2,256,256]{3,2,1,0:T(8,128)} %param.24) | copy-start | bytes 3145732
  197.8 114.5 %collective-permute-start.6 = (bf16[2,384,256]{2,1,0:T(8,128)(2,1)}, bf16[2,384,256]{2,1,0:T(8,128)(2,1)S(1)}, u32[]{:S(2)}, u32[]{:S(2)}) collective-permute-start(bf16[2,384,256]{2,1,0:T(8,128)(2,1)} %slice.470), channel_id=1, source_target_pairs={{0,30},{2,0},{4,2},{6,4},{8,6},{10,8},{12,10},{14,12},{16,14},{18,... | collective-permute-start | bytes 1179656 | tf_op jit(solution)/shard_map/ppermute | solution.py:16
  203.3 109.8 %collective-permute-start.7 = (bf16[2,256,384]{2,1,0:T(8,128)(2,1)}, bf16[2,256,384]{2,1,0:T(8,128)(2,1)}, u32[]{:S(2)}, u32[]{:S(2)}) collective-permute-start(bf16[2,256,384]{2,1,0:T(8,128)(2,1)} %slice.471), channel_id=1, source_target_pairs={{0,16},{2,18},{4,20},{6,22},{8,24},{10,26},{12,28},{14,30},{16,0},... | collective-permute-start | bytes 1179656 | tf_op jit(solution)/shard_map/ppermute | solution.py:16
  203.3 109.0 %collective-permute-start.8 = (bf16[2,256,256]{2,1,0:T(8,128)(2,1)}, bf16[2,256,256]{2,1,0:T(8,128)(2,1)}, u32[]{:S(2)}, u32[]{:S(2)}) collective-permute-start(bf16[2,256,256]{2,1,0:T(8,128)(2,1)} %slice.472), channel_id=1, source_target_pairs={{0,14},{2,16},{4,18},{6,20},{8,22},{10,24},{12,26},{14,28},{16,30}... | collective-permute-start | bytes 786440 | tf_op jit(solution)/shard_map/ppermute | solution.py:16
  312.2 152.7 %all-reduce.7.cloned.1.call-start = ((), (), s32[]{:S(2)}) async-start(), calls=%async_computation.6 | async-start | bytes 1179648 | tf_op jit(solution)/shard_map/psum | solution.py:159
  407.7 20.1 %copy-start = (f32[2,640,640]{2,1,0:T(8,128)S(1)}, f32[2,640,640]{2,1,0:T(8,128)}, u32[]{:S(2)}) copy-start(f32[2,640,640]{2,1,0:T(8,128)} %get-tuple-element.233) | copy-start | bytes 9830404
  410.0 17.8 %collective-permute-start.9 = (bf16[2,256,384]{2,1,0:T(8,128)(2,1)S(1)}, bf16[2,256,384]{2,1,0:T(8,128)(2,1)S(1)}, u32[]{:S(2)}, u32[]{:S(2)}) collective-permute-start(bf16[2,256,384]{2,1,0:T(8,128)(2,1)S(1)} %slice.484), channel_id=1, source_target_pairs={{0,16},{2,18},{4,20},{6,22},{8,24},{10,26},{12,28},{14,30},{16,0},... | collective-permute-start | bytes 1179656 | tf_op jit(solution)/shard_map/ppermute | solution.py:16
  410.1 18.0 %collective-permute-start.10 = (bf16[2,256,256]{2,1,0:T(8,128)(2,1)S(1)}, bf16[2,256,256]{2,1,0:T(8,128)(2,1)S(1)}, u32[]{:S(2)}, u32[]{:S(2)}) collective-permute-start(bf16[2,256,256]{2,1,0:T(8,128)(2,1)S(1)} %slice.486), channel_id=1, source_target_pairs={{0,18},{2,20},{4,22},{6,24},{8,26},{10,28},{12,30},{14,0},{16,2},{... | collective-permute-start | bytes 786440 | tf_op jit(solution)/shard_map/ppermute | solution.py:16
  428.1 19.9 %copy-start.22 = (bf16[4,256,256]{2,1,0:T(8,128)(2,1)S(1)}, bf16[4,256,256]{2,1,0:T(8,128)(2,1)}, u32[]{:S(2)}) copy-start(bf16[4,256,256]{2,1,0:T(8,128)(2,1)} %get-tuple-element.254) | copy-start | bytes 1572868
  428.2 18.8 %collective-permute-start.11 = (bf16[2,384,256]{2,1,0:T(8,128)(2,1)S(1)}, bf16[2,384,256]{2,1,0:T(8,128)(2,1)S(1)}, u32[]{:S(2)}, u32[]{:S(2)}) collective-permute-start(bf16[2,384,256]{2,1,0:T(8,128)(2,1)S(1)} %slice.530), channel_id=1, source_target_pairs={{0,2},{2,4},{4,6},{6,8},{8,10},{10,12},{12,14},{14,16},{16,18},{18... | collective-permute-start | bytes 1179656 | tf_op jit(solution)/shard_map/ppermute | solution.py:16
  448.0 29.3 %reduce-scatter.5.cloned.1.call-start = ((), (), s32[]{:S(2)}) async-start(), calls=%async_computation.7 | async-start | bytes 1572864 | tf_op jit(solution)/shard_map/reduce_scatter | solution.py:134
  449.1 119.2 %copy-start.3 = (f32[2,2,256,256]{3,2,1,0:T(8,128)S(1)}, f32[2,2,256,256]{3,2,1,0:T(8,128)}, u32[]{:S(2)}) copy-start(f32[2,2,256,256]{3,2,1,0:T(8,128)} %multiply_subtract_fusion.1) | copy-start | bytes 3145732
  (30 other events, 136.1 us)
Sparse Core Ops, SparseCore 0:
  17.1 9.6 all-gather.3
  175.9 18.3 all-reduce.4
  197.1 9.5 reduce-scatter.2
  312.3 7.9 all-gather.5
  448.1 16.7 all-reduce.6
  467.6 9.5 reduce-scatter.4
where the time goes:
time: 582 us; the launch traced here: 576 us
  blocking collectives  196 us (34%)
  waiting for transfers between devices  129 us (22%)
  local copies, waits for them, and re-layouts  108 us (19%)
  other arithmetic  61 us (10%)
  starting transfers between devices  28.5 us (5%)
  matrix products  22 us (4%)
  loops' own time  15.8 us (3%)
  between operations  15.8 us (3%)
    psum x2, blocking collectives, body(): probe_grad = lax.psum(probe_updates, 'tile')  194 us
    ppermute x12, waiting for transfers between devices, shifted(): lax.ppermute(array, axis, [(i, (i + by) % peers) for i in range(peers)])  83.9 us
    psum x2, waiting for transfers between devices, body(): lax.psum(tile_grad.astype(jnp.bfloat16), 'mode').astype(jnp.float32)  33.1 us
    ppermute x12, starting transfers between devices, shifted(): lax.ppermute(array, axis, [(i, (i + by) % peers) for i in range(peers)])  28.2 us
    dynamic_update_slice x4, local copies, waits for them, and re-layouts, place(): return lax.dynamic_update_slice(acc, current + object_terms[slot], where)  26.3 us
    another operation x7, other arithmetic  20.1 us
    gather x24, local copies, waits for them, and re-layouts  19.3 us
    dot_general x4, matrix products, transform(): jnp.einsum('ij,bjk->bik', left, field.reshape(count, 2 * length, length),...  16.8 us
  transfers between devices with their start and end apart: 18, of which 10 were waited for; matrix products, arithmetic and copies ran while one was open for 8% of the time, Pallas kernels for 0%

commit v1 on v0

--- a/solution.py
+++ b/solution.py
@@ -157,7 +157,7 @@
         )
         tile_grad = gradient[:, :tile, :tile].at[:, :, :patch].add(from_left)
         tile_grad = lax.psum(tile_grad.astype(jnp.bfloat16), "mode").astype(jnp.float32)
-        probe_grad = lax.psum(probe_updates, "tile")
+        probe_grad = jnp.sum(lax.all_gather(probe_updates, "tile"), axis=0)
         state = state - step_object * tile_grad
         probe_now = probe_now - step_probe / positions * probe_grad
     return (state[None], probe_now)

time: 582 us -> 802 us (1.38)
  waiting for transfers between devices: 129 us -> 521 us
  blocking collectives: 196 us -> 2.09 us
  other arithmetic: 61 us -> 76 us
    all_gather x0 -> x2, waiting for transfers between devices: none -> 399 us  [body(): probe_grad = jnp.sum(lax.all_gather(probe_updates, 'tile'), axis=0)]
    psum x2 -> x0, blocking collectives: 194 us -> none  [body(): probe_grad = lax.psum(probe_updates, 'tile')]
    reduce_sum x0 -> x2, other arithmetic: none -> 14.1 us  [body(): probe_grad = jnp.sum(lax.all_gather(probe_updates, 'tile'), axis=0)]
    reduce_scatter x2 -> x0, waiting for transfers between devices: 12.3 us -> none  [body(): lax.psum_scatter(probe_updates.astype(jnp.bfloat16), 'mode', scatter_dime...]
  transfers between devices with their start and end apart: 18 -> 18, of which waited for: 10 -> 10; matrix products, arithmetic and copies ran while one was open for 8% -> 6% of each run, Pallas kernels for 0% -> 0%
where the time goes in v1:
time: 802 us; the launch traced here: 797 us
  waiting for transfers between devices  521 us (65%)
  local copies, waits for them, and re-layouts  110 us (14%)
  other arithmetic  76 us (9%)
  starting transfers between devices  32.6 us (4%)
  matrix products  22.1 us (3%)
  between operations  16.4 us (2%)
  loops' own time  15.8 us (2%)
    all_gather x2, waiting for transfers between devices, body(): probe_grad = jnp.sum(lax.all_gather(probe_updates, 'tile'), axis=0)  399 us
    ppermute x12, waiting for transfers between devices, shifted(): lax.ppermute(array, axis, [(i, (i + by) % peers) for i in range(peers)])  85.1 us
    psum x2, waiting for transfers between devices, body(): lax.psum(tile_grad.astype(jnp.bfloat16), 'mode').astype(jnp.float32)  37.6 us
    ppermute x12, starting transfers between devices, shifted(): lax.ppermute(array, axis, [(i, (i + by) % peers) for i in range(peers)])  32.3 us
    dynamic_update_slice x4, local copies, waits for them, and re-layouts, place(): return lax.dynamic_update_slice(acc, current + object_terms[slot], where)  26.3 us
    gather x24, local copies, waits for them, and re-layouts  20.2 us
    another operation x7, other arithmetic  20.1 us
    dot_general x4, matrix products, transform(): jnp.einsum('ij,bjk->bik', left, field.reshape(count, 2 * length, length),...  16.9 us
  transfers between devices with their start and end apart: 18, of which 10 were waited for; matrix products, arithmetic and copies ran while one was open for 6% of the time, Pallas kernels for 0%

profile of v1, /device:TPU:0, one launch (start us, length us, event | category | flops | bytes accessed | tf_op | source)
XLA Modules:
  0.0 796.7 jit_solution(13131660799891368798)
XLA Ops:
  8.6 7.0 collective-permute-start
  25.1 17.7 %collective-permute-done.2 = bf16[2,256,256]{2,1,0:T(8,128)(2,1)S(1)} collective-permute-done((bf16[2,256,256]{2,1,0:T(8,128)(2,1)S(1)}, bf16[2,256,256]{2,1,0:T(8,128)(2,1)S(1)}, u32[]{:S(2)}, u32[]{:S(2)}) %collective-permute-start.2) | collective-permute-done | bytes 262176 | tf_op jit(solution)/shard_map/ppermute | solution.py:16
  46.6 8.0 %while.36 = (s32[]{:T(128)}, bf16[2,640,640]{2,1,0:T(8,128)(2,1)S(1)}, s32[4,3]{1,0:T(4,128)S(1)}, bf16[4,2,256,256]{3,2,1,0:T(8,128)(2,1)S(1)}, s32[]{:T(128)}) while((s32[]{:T(128)}, bf16[2,640,640]{2,1,0:T(8,128)(2,1)S(1)}, s32[4,3]{1,0:T(4,128)S(1)}, bf16[4,2,256,256]{3,2,1,0:T(8,128)(2,1)S(1)}, s32[]{:T(128)}) %tuple.140), condition=%wide.while_cond.6, body=%wide.while_body.6.sunk | while | flops 2 | bytes 524405 | solution.py:109
  60.4 5.5 subtract_convert_fusion.1
  108.0 24.8 %while.34 = (s32[]{:T(128)}, f32[2,640,640]{2,1,0:T(8,128)}, s32[2,2]{1,0:T(2,128)S(1)}, f32[2,2,256,256]{3,2,1,0:T(8,128)S(1)}, s32[]{:T(128)}, /*index=5*/s32[]{:T(128)}, s32[]{:T(128)}) while((s32[]{:T(128)}, f32[2,640,640]{2,1,0:T(8,128)}, s32[2,2]{1,0:T(2,128)S(1)}, f32[2,2,256,256]{3,2,1,0:T(8,128)S(1)}, s32[]{:T(128)}, ...), condition=%wide.region_4.5_spmd, body=%wide.region_3.4_spmd.sunk | while | flops 131080 | bytes 2621637 | solution.py:146
  113.8 6.4 dynamic_update_slice.16
  126.0 6.8 dynamic_update_slice.16
  136.5 24.7 %collective-permute-done.3 = bf16[2,256,384]{2,1,0:T(8,128)(2,1)S(1)} collective-permute-done((bf16[2,256,384]{2,1,0:T(8,128)(2,1)S(1)}, bf16[2,256,384]{2,1,0:T(8,128)(2,1)S(1)}, u32[]{:S(2)}, u32[]{:S(2)}) %collective-permute-start.3) | collective-permute-done | bytes 393248 | tf_op jit(solution)/shard_map/ppermute | solution.py:16
  161.6 5.9 collective-permute-start.5
  168.6 6.6 collective-permute-done.5
  177.4 19.0 %all-reduce.9.cloned.1.call-done = (bf16[2,384,384]{2,1,0:T(8,128)(2,1)}, bf16[4,2,256,256]{3,2,0,1:T(8,128)(2,1)}) async-done(((bf16[2,384,384]{2,1,0:T(8,128)(2,1)}, bf16[4,2,256,256]{3,2,0,1:T(8,128)(2,1)}), (bf16[2,384,384]{2,1,0:T(8,128)(2,1)}, bf16[4,2,256,256]{3,2,0,1:T(8,128)(2,1)})) %all-reduce.9.cloned.1.call-update) | async-done | bytes 1638416 | tf_op jit(solution)/shard_map/psum | solution.py:159
  207.7 206.6 %all-gather.12.cloned.1.call-done = f32[32,2,256,256]{3,2,0,1:T(8,128)} async-done(((f32[2,2,256,256]{3,2,0,1:T(8,128)}), f32[32,2,256,256]{3,2,0,1:T(8,128)}) %all-gather.12.cloned.1.call-update) | async-done | bytes 16777232 | tf_op jit(solution)/shard_map/all_gather | solution.py:160
  414.3 7.0 reduce_sum.113
  427.3 12.6 %while.37 = (s32[]{:T(128)}, bf16[2,640,640]{2,1,0:T(8,128)(2,1)}, s32[4,3]{1,0:T(4,128)S(1)}, bf16[4,2,256,256]{3,2,1,0:T(8,128)(2,1)S(1)}, s32[]{:T(128)}) while((s32[]{:T(128)}, bf16[2,640,640]{2,1,0:T(8,128)(2,1)}, s32[4,3]{1,0:T(4,128)S(1)}, bf16[4,2,256,256]{3,2,1,0:T(8,128)(2,1)S(1)}, s32[]{:T(128)}) %tuple.166), condition=%wide.while_cond.7, body=%wide.while_body.7.sunk | while | flops 2 | bytes 524405 | solution.py:109
  447.0 5.7 subtract_convert_fusion
  494.8 24.8 %while.35 = (s32[]{:T(128)}, f32[2,640,640]{2,1,0:T(8,128)}, s32[2,2]{1,0:T(2,128)S(1)}, f32[2,2,256,256]{3,2,1,0:T(8,128)S(1)}, s32[]{:T(128)}, /*index=5*/s32[]{:T(128)}, s32[]{:T(128)}) while((s32[]{:T(128)}, f32[2,640,640]{2,1,0:T(8,128)}, s32[2,2]{1,0:T(2,128)S(1)}, f32[2,2,256,256]{3,2,1,0:T(8,128)S(1)}, s32[]{:T(128)}, ...), condition=%wide.region_14.15_spmd, body=%wide.region_13.14_spmd.sunk | while | flops 131080 | bytes 2621637 | solution.py:146
  500.6 6.4 dynamic_update_slice.17
  512.8 6.8 dynamic_update_slice.17
  525.5 20.9 %collective-permute-done.9 = bf16[2,256,384]{2,1,0:T(8,128)(2,1)S(1)} collective-permute-done((bf16[2,256,384]{2,1,0:T(8,128)(2,1)S(1)}, bf16[2,256,384]{2,1,0:T(8,128)(2,1)S(1)}, u32[]{:S(2)}, u32[]{:S(2)}) %collective-permute-start.9) | collective-permute-done | bytes 393248 | tf_op jit(solution)/shard_map/ppermute | solution.py:16
  546.8 6.8 collective-permute-start.11
  554.7 11.6 %collective-permute-done.11 = bf16[2,384,256]{2,1,0:T(8,128)(2,1)S(1)} collective-permute-done((bf16[2,384,256]{2,1,0:T(8,128)(2,1)S(1)}, bf16[2,384,256]{2,1,0:T(8,128)(2,1)S(1)}, u32[]{:S(2)}, u32[]{:S(2)}) %collective-permute-start.11) | collective-permute-done | bytes 393248 | tf_op jit(solution)/shard_map/ppermute | solution.py:16
  567.3 18.6 %all-reduce.7.cloned.1.call-done = (bf16[2,384,384]{2,1,0:T(8,128)(2,1)}, bf16[4,2,256,256]{3,2,0,1:T(8,128)(2,1)}) async-done(((bf16[2,384,384]{2,1,0:T(8,128)(2,1)}, bf16[4,2,256,256]{3,2,0,1:T(8,128)(2,1)}), (bf16[2,384,384]{2,1,0:T(8,128)(2,1)}, bf16[4,2,256,256]{3,2,0,1:T(8,128)(2,1)})) %all-reduce.7.cloned.1.call-update) | async-done | bytes 1638416 | tf_op jit(solution)/shard_map/psum | solution.py:159
  589.3 192.0 %all-gather.14.cloned.1.call-done = f32[32,2,256,256]{3,2,0,1:T(8,128)} async-done(((f32[2,2,256,256]{3,2,0,1:T(8,128)}), f32[32,2,256,256]{3,2,0,1:T(8,128)}) %all-gather.14.cloned.1.call-update) | async-done | bytes 16777232 | tf_op jit(solution)/shard_map/all_gather | solution.py:160
  781.4 7.1 reduce_sum.119
  (245 shorter events, 175.5 us)
Async XLA Ops:
  7.2 49.8 %all-gather.8.cloned.1.call-start = ((), (), s32[]{:S(2)}) async-start(), calls=%async_computation | async-start | bytes 3145728 | tf_op jit(solution)/shard_map/all_gather | solution.py:120
  8.6 34.2 %collective-permute-start = (bf16[2,384,256]{2,1,0:T(8,128)(2,1)S(1)}, bf16[2,384,256]{2,1,0:T(8,128)(2,1)S(1)}, u32[]{:S(2)}, u32[]{:S(2)}) collective-permute-start(bf16[2,384,256]{2,1,0:T(8,128)(2,1)S(1)} %slice.449), channel_id=1, source_target_pairs={{0,30},{2,0},{4,2},{6,4},{8,6},{10,8},{12,10},{14,12},{16,14},{18,... | collective-permute-start | bytes 1179656 | tf_op jit(solution)/shard_map/ppermute | solution.py:16
  15.7 30.7 %collective-permute-start.1 = (bf16[2,256,384]{2,1,0:T(8,128)(2,1)S(1)}, bf16[2,256,384]{2,1,0:T(8,128)(2,1)S(1)}, u32[]{:S(2)}, u32[]{:S(2)}) collective-permute-start(bf16[2,256,384]{2,1,0:T(8,128)(2,1)S(1)} %slice.450), channel_id=1, source_target_pairs={{0,16},{2,18},{4,20},{6,22},{8,24},{10,26},{12,28},{14,30},{16,0},... | collective-permute-start | bytes 1179656 | tf_op jit(solution)/shard_map/ppermute | solution.py:16
  15.8 27.0 %collective-permute-start.2 = (bf16[2,256,256]{2,1,0:T(8,128)(2,1)S(1)}, bf16[2,256,256]{2,1,0:T(8,128)(2,1)S(1)}, u32[]{:S(2)}, u32[]{:S(2)}) collective-permute-start(bf16[2,256,256]{2,1,0:T(8,128)(2,1)S(1)} %slice.451), channel_id=1, source_target_pairs={{0,14},{2,16},{4,18},{6,20},{8,22},{10,24},{12,26},{14,28},{16,30}... | collective-permute-start | bytes 786440 | tf_op jit(solution)/shard_map/ppermute | solution.py:16
  16.9 179.5 %all-reduce.9.cloned.1.call-start = ((), (), s32[]{:S(2)}) async-start(), calls=%async_computation.5 | async-start | bytes 3276800 | tf_op jit(solution)/shard_map/psum | solution.py:159
  132.8 28.4 %copy-start = (f32[2,640,640]{2,1,0:T(8,128)S(1)}, f32[2,640,640]{2,1,0:T(8,128)}, u32[]{:S(2)}) copy-start(f32[2,640,640]{2,1,0:T(8,128)} %get-tuple-element.232) | copy-start | bytes 9830404
  135.1 26.1 %collective-permute-start.3 = (bf16[2,256,384]{2,1,0:T(8,128)(2,1)S(1)}, bf16[2,256,384]{2,1,0:T(8,128)(2,1)S(1)}, u32[]{:S(2)}, u32[]{:S(2)}) collective-permute-start(bf16[2,256,384]{2,1,0:T(8,128)(2,1)S(1)} %slice.463), channel_id=1, source_target_pairs={{0,16},{2,18},{4,20},{6,22},{8,24},{10,26},{12,28},{14,30},{16,0},... | collective-permute-start | bytes 1179656 | tf_op jit(solution)/shard_map/ppermute | solution.py:16
  135.2 32.3 %copy-start.24 = (bf16[4,256,256]{2,1,0:T(8,128)(2,1)S(1)}, bf16[4,256,256]{2,1,0:T(8,128)(2,1)}, u32[]{:S(2)}) copy-start(bf16[4,256,256]{2,1,0:T(8,128)(2,1)} %get-tuple-element.259) | copy-start | bytes 1572868
  135.2 26.2 %collective-permute-start.4 = (bf16[2,256,256]{2,1,0:T(8,128)(2,1)S(1)}, bf16[2,256,256]{2,1,0:T(8,128)(2,1)S(1)}, u32[]{:S(2)}, u32[]{:S(2)}) collective-permute-start(bf16[2,256,256]{2,1,0:T(8,128)(2,1)S(1)} %slice.465), channel_id=1, source_target_pairs={{0,18},{2,20},{4,22},{6,24},{8,26},{10,28},{12,30},{14,0},{16,2},{... | collective-permute-start | bytes 786440 | tf_op jit(solution)/shard_map/ppermute | solution.py:16
  161.6 13.6 %collective-permute-start.5 = (bf16[2,384,256]{2,1,0:T(8,128)(2,1)S(1)}, bf16[2,384,256]{2,1,0:T(8,128)(2,1)S(1)}, u32[]{:S(2)}, u32[]{:S(2)}) collective-permute-start(bf16[2,384,256]{2,1,0:T(8,128)(2,1)S(1)} %slice.531), channel_id=1, source_target_pairs={{0,2},{2,4},{4,6},{6,8},{8,10},{10,12},{12,14},{14,16},{16,18},{18... | collective-permute-start | bytes 1179656 | tf_op jit(solution)/shard_map/ppermute | solution.py:16
  175.3 23.3 %copy-start.2 = (f32[1,2,384,384]{3,2,1,0:T(8,128)S(1)}, f32[1,2,384,384]{3,2,1,0:T(8,128)}, u32[]{:S(2)}) copy-start(f32[1,2,384,384]{3,2,1,0:T(8,128)} %param.23) | copy-start | bytes 3538948
  176.1 238.2 %all-gather.12.cloned.1.call-start = ((), (), s32[]{:S(2)}) async-start(), calls=%async_computation.2 | async-start | bytes 17825792 | tf_op jit(solution)/shard_map/all_gather | solution.py:160
  198.6 243.7 %all-gather.10.cloned.1.call-start = ((), (), s32[]{:S(2)}) async-start(), calls=%async_computation.1 | async-start | bytes 3145728 | tf_op jit(solution)/shard_map/all_gather | solution.py:120
  201.1 223.6 %collective-permute-start.6 = (bf16[2,384,256]{2,1,0:T(8,128)(2,1)}, bf16[2,384,256]{2,1,0:T(8,128)(2,1)S(1)}, u32[]{:S(2)}, u32[]{:S(2)}) collective-permute-start(bf16[2,384,256]{2,1,0:T(8,128)(2,1)} %slice.470), channel_id=1, source_target_pairs={{0,30},{2,0},{4,2},{6,4},{8,6},{10,8},{12,10},{14,12},{16,14},{18,... | collective-permute-start | bytes 1179656 | tf_op jit(solution)/shard_map/ppermute | solution.py:16
  206.6 218.2 %collective-permute-start.7 = (bf16[2,256,384]{2,1,0:T(8,128)(2,1)}, bf16[2,256,384]{2,1,0:T(8,128)(2,1)}, u32[]{:S(2)}, u32[]{:S(2)}) collective-permute-start(bf16[2,256,384]{2,1,0:T(8,128)(2,1)} %slice.471), channel_id=1, source_target_pairs={{0,16},{2,18},{4,20},{6,22},{8,24},{10,26},{12,28},{14,30},{16,0},... | collective-permute-start | bytes 1179656 | tf_op jit(solution)/shard_map/ppermute | solution.py:16
  206.6 218.2 %collective-permute-start.8 = (bf16[2,256,256]{2,1,0:T(8,128)(2,1)}, bf16[2,256,256]{2,1,0:T(8,128)(2,1)}, u32[]{:S(2)}, u32[]{:S(2)}) collective-permute-start(bf16[2,256,256]{2,1,0:T(8,128)(2,1)} %slice.472), channel_id=1, source_target_pairs={{0,14},{2,16},{4,18},{6,20},{8,22},{10,24},{12,26},{14,28},{16,30}... | collective-permute-start | bytes 786440 | tf_op jit(solution)/shard_map/ppermute | solution.py:16
  424.7 161.1 %all-reduce.7.cloned.1.call-start = ((), (), s32[]{:S(2)}) async-start(), calls=%async_computation.4 | async-start | bytes 3276800 | tf_op jit(solution)/shard_map/psum | solution.py:159
  519.6 26.8 %copy-start.1 = (f32[2,640,640]{2,1,0:T(8,128)S(1)}, f32[2,640,640]{2,1,0:T(8,128)}, u32[]{:S(2)}) copy-start(f32[2,640,640]{2,1,0:T(8,128)} %get-tuple-element.233) | copy-start | bytes 9830404
  521.9 24.5 %collective-permute-start.9 = (bf16[2,256,384]{2,1,0:T(8,128)(2,1)S(1)}, bf16[2,256,384]{2,1,0:T(8,128)(2,1)S(1)}, u32[]{:S(2)}, u32[]{:S(2)}) collective-permute-start(bf16[2,256,384]{2,1,0:T(8,128)(2,1)S(1)} %slice.484), channel_id=1, source_target_pairs={{0,16},{2,18},{4,20},{6,22},{8,24},{10,26},{12,28},{14,30},{16,0},... | collective-permute-start | bytes 1179656 | tf_op jit(solution)/shard_map/ppermute | solution.py:16
  523.4 30.2 %copy-start.23 = (bf16[4,256,256]{2,1,0:T(8,128)(2,1)S(1)}, bf16[4,256,256]{2,1,0:T(8,128)(2,1)}, u32[]{:S(2)}) copy-start(bf16[4,256,256]{2,1,0:T(8,128)(2,1)} %get-tuple-element.257) | copy-start | bytes 1572868
  523.4 23.3 %collective-permute-start.10 = (bf16[2,256,256]{2,1,0:T(8,128)(2,1)S(1)}, bf16[2,256,256]{2,1,0:T(8,128)(2,1)S(1)}, u32[]{:S(2)}, u32[]{:S(2)}) collective-permute-start(bf16[2,256,256]{2,1,0:T(8,128)(2,1)S(1)} %slice.486), channel_id=1, source_target_pairs={{0,18},{2,20},{4,22},{6,24},{8,26},{10,28},{12,30},{14,0},{16,2},{... | collective-permute-start | bytes 786440 | tf_op jit(solution)/shard_map/ppermute | solution.py:16
  546.8 19.5 %collective-permute-start.11 = (bf16[2,384,256]{2,1,0:T(8,128)(2,1)S(1)}, bf16[2,384,256]{2,1,0:T(8,128)(2,1)S(1)}, u32[]{:S(2)}, u32[]{:S(2)}) collective-permute-start(bf16[2,384,256]{2,1,0:T(8,128)(2,1)S(1)} %slice.530), channel_id=1, source_target_pairs={{0,2},{2,4},{4,6},{6,8},{8,10},{10,12},{12,14},{14,16},{16,18},{18... | collective-permute-start | bytes 1179656 | tf_op jit(solution)/shard_map/ppermute | solution.py:16
  566.4 21.6 %copy-start.22 = (bf16[2,384,384]{2,1,0:T(8,128)(2,1)S(1)}, bf16[2,384,384]{2,1,0:T(8,128)(2,1)}, u32[]{:S(2)}) copy-start(bf16[2,384,384]{2,1,0:T(8,128)(2,1)} %get-tuple-element.298) | copy-start | bytes 1769476
  567.3 214.1 %all-gather.14.cloned.1.call-start = ((), (), s32[]{:S(2)}) async-start(), calls=%async_computation.3 | async-start | bytes 17825792 | tf_op jit(solution)/shard_map/all_gather | solution.py:160
  (29 other events, 92.7 us)
Sparse Core Ops, SparseCore 0:
  17.1 9.6 all-gather.7
  176.3 20.1 all-reduce.8
  199.8 214.5 all-gather.11
  424.9 8.7 all-gather.9
  567.4 18.4 all-reduce.6
  589.1 192.2 all-gather.13
